TPU v7x, 32 devices: a whole 2x2x4 slice. The times are simulated.
32 devices in a mesh: ctx: 8 (over z, core), tp: 4 (over y, x).
Axes of the slice: x: 2, y: 2, z: 4, core: 2. Of those that a mesh axis runs over, the one named last changes fastest.
Arguments:
- hidden_rows: bfloat16 [4096, 8192], P('ctx', 'tp'), may hold values from -6 to 6
- w_value: bfloat16 [8192, 8192], P('ctx', 'tp'), may hold values from -0.0625 to 0.0625
- w_gate: bfloat16 [8192, 8192], P('ctx', 'tp'), may hold values from -0.0625 to 0.0625
- state_proj: bfloat16 [4096, 2, 4, 256], P('ctx'), may hold values from -1.5 to 1.5
- rates: float32 [4096, 128], P('ctx', 'tp'), may hold values from 0 to 4.5, as said below
- read_weights: float32 [6, 4096, 128], P(None, 'ctx', 'tp'), may hold values from 0.25 to 2
- prior_state: float32 [128, 64, 256], P('tp'), may hold values from -24 to 24
- skip_weight: float32 [128], P('tp'), may hold values from 0.5 to 2
- norm_gain: float32 [8192], P('tp'), may hold values from 0.25 to 1.75
Outputs:
- layer_out: bfloat16 [4096, 8192], P('ctx', 'tp')
Inputs may be any that keep to these rules, and one draw needn't show every extreme that they name: Positive rates.
All inputs are finite; a program needn't handle non-finite values.
Results may differ from a plain program's by a relative error of at most 0.0085.
Values may be sent and summed in bfloat16 or wider, within the bound.
A program may use at most 128 MiB of HBM per device.

v0:
```python
import jax
import jax.numpy as jnp
from jax import lax
from jax.sharding import PartitionSpec as P

HEAD_DIM = 64
STATE = 256
HPG = 32
LEVELS = 6


def swapped(value, axis, distance):
    return lax.ppermute(value, axis, [(i, i ^ 1 << distance) for i in range(lax.axis_size(axis))])


def on_device(
    hidden_rows,
    w_value,
    w_gate,
    state_proj,
    rates,
    read_weights,
    prior_state,
    skip_weight,
    norm_gain,
):
    tok_rows = rates.shape[0]
    head_count = rates.shape[1]
    level_total = LEVELS - 2
    full_rows = lax.all_gather(hidden_rows, "tp", axis=1, tiled=True)
    value_sum = jnp.dot(
        full_rows,
        lax.all_gather(w_value, "ctx", axis=0, tiled=True),
        preferred_element_type=jnp.float32,
    )
    gate_sum = jnp.dot(
        full_rows,
        lax.all_gather(w_gate, "ctx", axis=0, tiled=True),
        preferred_element_type=jnp.float32,
    )
    values_proj = value_sum.astype(jnp.bfloat16)
    gates_proj = gate_sum.astype(jnp.bfloat16)
    values3 = values_proj.reshape(tok_rows, head_count, HEAD_DIM)
    group_index = lax.axis_index("tp") * head_count // HPG
    write_vec = lax.dynamic_index_in_dim(state_proj[:, 0], group_index, 1, keepdims=False)
    read_vec = lax.dynamic_index_in_dim(state_proj[:, 1], group_index, 1, keepdims=False)
    cum_rate = jnp.cumsum(rates, axis=0)
    scores = lax.dot_general(
        read_vec, write_vec, (((1,), (1,)), ((), ())), preferred_element_type=jnp.float32
    )
    rate_lag = cum_rate.T[:, :, None] - cum_rate.T[:, None, :]
    causal = (jnp.arange(tok_rows)[:, None] >= jnp.arange(tok_rows)[None, :])[None]
    mixing = (
        jnp.where(causal, jnp.exp(-jnp.where(causal, rate_lag, 0.0)), 0.0) * scores[None]
    ).astype(jnp.bfloat16)
    local_out = jnp.einsum("hts,shp->thp", mixing, values3, preferred_element_type=jnp.float32)
    span_total = cum_rate[-1]
    write_weighted = (
        jnp.exp(-(span_total[None] - cum_rate))[:, :, None]
        * write_vec[:, None, :].astype(jnp.float32)
    ).astype(jnp.bfloat16)
    end_state = jnp.einsum(
        "thn,thp->hpn", write_weighted, values3, preferred_element_type=jnp.float32
    )
    my_block = lax.axis_index("ctx")
    agg_state = end_state
    agg_rate = span_total
    start_rate = jnp.zeros((head_count,), jnp.float32)
    tier_components = []
    for bit_pos in range(lax.axis_size("ctx").bit_length() - 1):
        other_state, other_rate = swapped((agg_state, agg_rate), "ctx", bit_pos)
        is_upper = jnp.right_shift(my_block, bit_pos) % 2 == 1
        tier_components.append(
            jnp.where(is_upper, other_state * jnp.exp(-start_rate)[:, None, None], 0.0)
        )
        agg_state = jnp.where(
            is_upper,
            other_state * jnp.exp(-agg_rate)[:, None, None] + agg_state,
            agg_state * jnp.exp(-other_rate)[:, None, None] + other_state,
        )
        agg_rate = agg_rate + other_rate
        start_rate = jnp.where(is_upper, start_rate + other_rate, start_rate)
    for extra_level in range(level_total - len(tier_components)):
        tier_components.append(jnp.zeros((head_count, HEAD_DIM, STATE), jnp.float32))
    carried = jnp.stack(tier_components)
    prior_part = jnp.exp(-start_rate)[:, None, None] * prior_state
    states = jnp.concatenate([carried, prior_part[None]], axis=0)
    projected = jnp.einsum(
        "tn,lhpn->tlhp", read_vec.astype(jnp.float32), states, precision=lax.Precision.HIGHEST
    )
    read_scale = read_weights[1:] * jnp.exp(-cum_rate)[None]
    carried_out = jnp.einsum(
        "lth,tlhp->thp", read_scale, projected, precision=lax.Precision.HIGHEST
    )
    mixed_out = (
        read_weights[0][:, :, None] * local_out
        + carried_out
        + skip_weight[None, :, None] * values3.astype(jnp.float32)
    )
    gates3 = gates_proj.reshape(tok_rows, head_count, HEAD_DIM).astype(jnp.float32)
    filtered_result = mixed_out * jax.nn.silu(gates3)
    inverse = lax.rsqrt(jnp.mean(filtered_result * filtered_result, axis=2, keepdims=True) + 1e-05)
    result = filtered_result * inverse * norm_gain.reshape(head_count, HEAD_DIM)[None]
    return result.reshape(tok_rows, head_count * HEAD_DIM).astype(jnp.bfloat16)


def solution(mesh):
    in_specs = (
        P("ctx", "tp"),
        P("ctx", "tp"),
        P("ctx", "tp"),
        P("ctx", None, None, None),
        P("ctx", "tp"),
        P(None, "ctx", "tp"),
        P("tp", None, None),
        P("tp"),
        P("tp"),
    )
    out_specs = P("ctx", "tp")
    return jax.shard_map(
        on_device, mesh=mesh, in_specs=in_specs, out_specs=out_specs, check_vma=False
    )
```

profile of v0, /device:TPU:17, one launch (start us, length us, event | category | flops | bytes accessed | tf_op | source)
XLA Modules:
  0.0 836.5 jit_solution(6695829626215990275)
XLA Ops:
  6.5 0.7 all-gather.4.cloned.1.call-update
  7.3 0.7 all-gather.6.cloned.1.call-update
  8.1 0.7 all-gather.8.cloned.1.call-update
  8.8 1.2 reduce-window.6
  10.2 0.7 copy_bitcast_fusion.2
  11.1 0.7 fusion.19
  11.8 1.1 constant_dynamic-slice_fusion
  12.9 0.7 negate_exponential_fusion
  13.6 0.9 fusion.12
  14.5 83.1 %all-gather.4.cloned.1.call-done = bf16[512,8192]{1,0:T(8,128)(2,1)} async-done(((bf16[512,2048]{1,0:T(8,128)(2,1)}), bf16[512,8192]{1,0:T(8,128)(2,1)}) %all-gather.4.cloned.1.call-update) | async-done | bytes 8388624 | tf_op jit(solution)/shard_map/all_gather | solution.py:30
  97.6 289.0 %all-gather.6.cloned.1.call-done = bf16[8192,2048]{1,0:T(8,128)(2,1)} async-done(((bf16[1024,2048]{1,0:T(8,128)(2,1)}), bf16[8192,2048]{1,0:T(8,128)(2,1)}) %all-gather.6.cloned.1.call-update) | async-done | bytes 33554448 | tf_op jit(solution)/shard_map/all_gather | solution.py:33
  386.6 25.6 %convolution_convert_fusion.1 = bf16[512,2048]{1,0:T(8,128)(2,1)} fusion(bf16[512,8192]{1,0:T(8,128)(2,1)} %all-gather.4.cloned.1.call-done, bf16[8192,2048]{1,0:T(8,128)(2,1)} %all-gather.6.cloned.1.call-done), kind=kOutput, calls=%fused_computation.16 | convolution fusion | flops 17180917760 | bytes 44040192 | tf_op jit(solution)/shard_map/dot_general | solution.py:31
  412.2 2.9 copy.27
  415.1 1.3 copy-done.6
  416.4 5.1 fusion.2
  421.5 0.3 collective-permute-start
  421.8 0.2 collective-permute-start.1
  422.0 3.9 collective-permute-done.1
  425.9 0.5 negate_exponential_fusion.4
  426.4 3.0 collective-permute-done.3
  429.4 0.6 add.71
  430.0 1.7 collective-permute-start.5
  431.7 2.3 collective-permute-done.5
  434.0 1.2 fusion.16
  435.3 1.3 copy-done.2
  436.6 3.4 add_select_fusion.1
  440.0 2.6 collective-permute-start.2
  442.6 0.8 mul.166
  443.4 0.8 iota_compare_fusion
  444.1 0.6 slice_bitcast_fusion
  444.8 1.6 multiply_bitcast_fusion
  446.4 1.3 fusion.10
  447.7 0.7 negate_exponential_fusion.2
  448.3 188.4 %collective-permute-done.2 = f32[32,64,256]{2,1,0:T(8,128)S(1)} collective-permute-done((f32[32,64,256]{2,1,0:T(8,128)}, f32[32,64,256]{2,1,0:T(8,128)S(1)}, u32[]{:S(2)}, u32[]{:S(2)}) %collective-permute-start.2) | collective-permute-done | bytes 2097184 | tf_op jit(solution)/shard_map/ppermute | solution.py:13
  636.8 3.4 add_select_fusion
  640.1 4.6 collective-permute-start.4
  644.7 120.0 %all-gather.8.cloned.1.call-done = bf16[8192,2048]{1,0:T(8,128)(2,1)} async-done(((bf16[1024,2048]{1,0:T(8,128)(2,1)}), bf16[8192,2048]{1,0:T(8,128)(2,1)}) %all-gather.8.cloned.1.call-update) | async-done | bytes 33554448 | tf_op jit(solution)/shard_map/all_gather | solution.py:38
  764.8 24.8 %fusion.8 = f32[512,2048]{1,0:T(8,128)} fusion(bf16[512,8192]{1,0:T(8,128)(2,1)} %all-gather.4.cloned.1.call-done, bf16[8192,2048]{1,0:T(8,128)(2,1)} %all-gather.8.cloned.1.call-done), kind=kOutput, calls=%fused_computation.15 | convolution fusion | flops 17181966336 | bytes 46137344 | tf_op jit(solution)/shard_map/dot_general | solution.py:36
  789.5 5.3 copy.32
  794.9 1.8 bitcast_dynamic-update-slice_fusion.3
  796.7 0.2 bitcast_dynamic-update-slice_fusion.2
  796.9 1.9 bitcast_dynamic-update-slice_fusion.1
  799.1 0.2 bitcast_dynamic-update-slice_fusion
  799.3 0.6 copy-done.10
  800.0 13.2 %multiply_reduce_fusion = f32[512,32,64]{0,2,1:T(8,128)} fusion(f32[512,32,5]{0,1,2:T(8,128)S(1)} %copy-done.10, f32[5,32,64,256]{3,2,1,0:T(8,128)S(1)} %bitcast_dynamic-update-slice_fusion, bf16[512,1,1,256]{3,2,1,0:T(2,128)(2,1)S(1)} %get-tuple-element.22), kind=kOutput, calls=%fused_computation.1 | convolution fusion | flops 16115564544 | bytes 15269888 | tf_op jit(solution)/shard_map/tn,lhpn->tlhp/dot_general | solution.py:88
  813.2 13.6 %multiply_reduce_fusion.1 = (f32[512,32]{0,1:T(8,128)S(1)}, f32[512,32,64]{0,2,1:T(8,128)S(1)}) fusion(f32[512,32,64]{0,2,1:T(8,128)S(1)} %bitcast.69, bf16[512,32,64]{0,2,1:T(8,128)(2,1)S(1)} %bitcast.71, f32[32]{0:T(128)S(1)} %copy-done.17, f32[512,32,64]{0,2,1:T(8,128)} %multiply_reduce_fusion, f32[512,512]{1,0:T(8,128)S(1)} %copy-done.8, ...), kind=kOutput, calls=%fused_computation.13 | convolution fusion | flops 1136640000 | bytes 16187520 | tf_op jit(solution)/shard_map/hts,shp->thp/dot_general | solution.py:56
  826.8 0.7 multiply_convert_fusion.4
  827.5 2.4 copy.33
  (46 shorter events, 0.8 us)
Async XLA Ops:
  6.5 2.2 copy-start
  6.5 91.1 %all-gather.4.cloned.1.call-start = ((), (), s32[]{:S(2)}) async-start(), calls=%async_computation | async-start | bytes 10485760 | tf_op jit(solution)/shard_map/all_gather | solution.py:30
  7.3 3.8 copy-start.4
  7.3 379.3 %all-gather.6.cloned.1.call-start = ((), (), s32[]{:S(2)}) async-start(), calls=%async_computation.1 | async-start | bytes 37748736 | tf_op jit(solution)/shard_map/all_gather | solution.py:33
  8.0 756.7 %all-gather.8.cloned.1.call-start = ((), (), s32[]{:S(2)}) async-start(), calls=%async_computation.2 | async-start | bytes 37748736 | tf_op jit(solution)/shard_map/all_gather | solution.py:38
  415.1 1.3 copy-start.6
  421.5 22.6 %copy-start.9 = (f32[6,512,32]{1,2,0:T(8,128)S(1)}, f32[6,512,32]{1,2,0:T(8,128)}, u32[]{:S(2)}) copy-start(f32[6,512,32]{1,2,0:T(8,128)} %param.14) | copy-start | bytes 1179652
  421.5 13.8 %collective-permute-start = (f32[32,64,256]{2,1,0:T(8,128)}, f32[32,64,256]{2,1,0:T(8,128)S(1)}, u32[]{:S(2)}, u32[]{:S(2)}) collective-permute-start(f32[32,64,256]{2,1,0:T(8,128)} %fusion.2), channel_id=1, source_target_pairs={{0,4},{4,0},{8,12},{12,8},{16,20},{20,16},{24,28},{28,24},{1,5},{5... | collective-permute-start | bytes 6291464 | tf_op jit(solution)/shard_map/ppermute | solution.py:13
  421.8 4.1 collective-permute-start.1
  426.4 3.0 collective-permute-start.3
  429.4 2.3 copy-start.16
  430.0 4.1 collective-permute-start.5
  435.3 1.3 copy-start.2
  440.0 196.8 %collective-permute-start.2 = (f32[32,64,256]{2,1,0:T(8,128)}, f32[32,64,256]{2,1,0:T(8,128)S(1)}, u32[]{:S(2)}, u32[]{:S(2)}) collective-permute-start(f32[32,64,256]{2,1,0:T(8,128)} %add_select_fusion.1), channel_id=1, source_target_pairs={{0,8},{4,12},{8,0},{12,4},{16,24},{20,28},{24,16},{28,20},{1,9},{5... | collective-permute-start | bytes 6291464 | tf_op jit(solution)/shard_map/ppermute | solution.py:13
  640.1 156.8 %collective-permute-start.4 = (f32[32,64,256]{2,1,0:T(8,128)}, f32[32,64,256]{2,1,0:T(8,128)}, u32[]{:S(2)}, u32[]{:S(2)}) collective-permute-start(f32[32,64,256]{2,1,0:T(8,128)} %add_select_fusion), channel_id=1, source_target_pairs={{0,16},{4,20},{8,24},{12,28},{16,0},{20,4},{24,8},{28,12},{1,17},{... | collective-permute-start | bytes 6291464 | tf_op jit(solution)/shard_map/ppermute | solution.py:13
  794.9 1.8 copy-start.15
  796.9 2.2 copy-start.5
  796.9 2.2 copy-start.14
  798.9 1.0 copy-start.10
  799.9 13.2 %copy-start.3 = (f32[512,2048]{0,1:T(8,128)S(1)}, f32[512,2048]{0,1:T(8,128)}, u32[]{:S(2)}) copy-start(f32[512,2048]{0,1:T(8,128)} %copy.32) | copy-start | bytes 12582916
  799.9 13.2 %copy-start.7 = (bf16[512,2048]{0,1:T(8,128)(2,1)S(1)}, bf16[512,2048]{0,1:T(8,128)(2,1)}, u32[]{:S(2)}) copy-start(bf16[512,2048]{0,1:T(8,128)(2,1)} %copy-done.6) | copy-start | bytes 6291460
  799.9 13.2 %copy-start.8 = (f32[512,512]{1,0:T(8,128)S(1)}, f32[512,512]{1,0:T(8,128)}, u32[]{:S(2)}) copy-start(f32[512,512]{1,0:T(8,128)} %fusion.10) | copy-start | bytes 3145732
  799.9 13.2 %copy-start.11 = (pred[512,512]{1,0:T(8,128)(4,1)S(1)}, pred[512,512]{1,0:T(8,128)(4,1)}, u32[]{:S(2)}) copy-start(pred[512,512]{1,0:T(8,128)(4,1)} %iota_compare_fusion) | copy-start | bytes 786436
  799.9 13.2 %copy-start.12 = (f32[32,512]{1,0:T(8,128)S(1)}, f32[32,512]{1,0:T(8,128)}, u32[]{:S(2)}) copy-start(f32[32,512]{1,0:T(8,128)} %get-tuple-element.11) | copy-start | bytes 196612
  799.9 13.2 %copy-start.13 = (f32[512,32]{0,1:T(8,128)S(1)}, f32[512,32]{0,1:T(8,128)}, u32[]{:S(2)}) copy-start(f32[512,32]{0,1:T(8,128)} %slice_bitcast_fusion) | copy-start | bytes 196612
  799.9 13.2 %copy-start.17 = (f32[32]{0:T(128)S(1)}, f32[32]{0:T(128)}, u32[]{:S(2)}) copy-start(f32[32]{0:T(128)} %param.16) | copy-start | bytes 388
  826.8 3.1 copy-start.1
Sparse Core Ops, SparseCore 0:
  9.2 88.3 all-gather.3
  99.2 287.3 all-gather.5
  388.2 376.4 all-gather.7
where the time goes:
time: 837 us; the launch traced here: 836 us
  waiting for transfers between devices  692 us (83%)
  matrix products  83.6 us (10%)
  other arithmetic  20.6 us (2%)
  local copies, waits for them, and re-layouts  17.6 us (2%)
  between operations  13.4 us (2%)
  starting transfers between devices  9.53 us (1%)
    all_gather x1, waiting for transfers between devices, on_device(): lax.all_gather(w_value, 'ctx', axis=0, tiled=True)  289 us
    ppermute x6, waiting for transfers between devices, swapped(): lax.ppermute(value, axis, [(i, i ^ 1 << distance) for i in range(lax.axis...  198 us
    all_gather x1, waiting for transfers between devices, on_device(): lax.all_gather(w_gate, 'ctx', axis=0, tiled=True)  120 us
    all_gather x1, waiting for transfers between devices, on_device(): full_rows = lax.all_gather(hidden_rows, 'tp', axis=1, tiled=True)  83.1 us
    dot_general x1, matrix products, on_device(): jnp.dot(full_rows, lax.all_gather(w_value, 'ctx', axis=0, tiled=True), pr...  25.6 us
    dot_general x1, matrix products, on_device(): jnp.dot(full_rows, lax.all_gather(w_gate, 'ctx', axis=0, tiled=True), pre...  24.8 us
  transfers between devices with their start and end apart: 9, of which 7 were waited for; matrix products, arithmetic and copies ran while one was open for 10% of the time, Pallas kernels for 0%

commit v1 on v0

--- a/solution.py
+++ b/solution.py
@@ -27,7 +27,17 @@
     tok_rows = rates.shape[0]
     head_count = rates.shape[1]
     level_total = LEVELS - 2
-    full_rows = lax.all_gather(hidden_rows, "tp", axis=1, tiled=True)
+    field = hidden_rows
+    kept_arr = jax.lax.psum(1, "tp")
+    high = jax.lax.axis_index("tp")
+    oldest, carry, low = (kept_arr, high, field.shape[1])
+    new = jnp.zeros([k * oldest if j0 == 1 else k for j0, k in enumerate(field.shape)], field.dtype)
+    full_rows = lax.dynamic_update_slice_in_dim(new, field, carry * low, axis=1)
+    for rr in [*range(1, oldest)]:
+        field = jax.lax.ppermute(field, "tp", [(j0, (j0 + 1) % oldest) for j0 in range(oldest)])
+        full_rows = lax.dynamic_update_slice_in_dim(
+            full_rows, field, (carry - rr) % oldest * low, axis=1
+        )
     value_sum = jnp.dot(
         full_rows,
         lax.all_gather(w_value, "ctx", axis=0, tiled=True),

time: 837 us -> 790 us (0.944)
  waiting for transfers between devices: 692 us -> 628 us
  local copies, waits for them, and re-layouts: 17.6 us -> 35.6 us
    all_gather x1, waiting for transfers between devices: 120 us -> 278 us  [on_device(): lax.all_gather(w_gate, 'ctx', axis=0, tiled=True)]
    all_gather x1, waiting for transfers between devices: 289 us -> 145 us  [on_device(): lax.all_gather(w_value, 'ctx', axis=0, tiled=True)]
    ppermute x0 -> x3, waiting for transfers between devices: none -> 121 us  [on_device(): jax.lax.ppermute(field, 'tp', [(j0, (j0 + 1) % oldest) for j0 in range(ol...]
    ppermute x6, waiting for transfers between devices: 198 us -> 81.2 us  [swapped(): lax.ppermute(value, axis, [(i, i ^ 1 << distance) for i in range(lax.axis...]
    all_gather x1 -> x0, waiting for transfers between devices: 83.1 us -> none  [on_device(): full_rows = lax.all_gather(hidden_rows, 'tp', axis=1, tiled=True)]
    dynamic_update_slice x0 -> x4, local copies, waits for them, and re-layouts: none -> 11.2 us  [the longest x3 9.73 us: on_device(): lax.dynamic_update_slice_in_dim(full_rows, field, (carry - rr) % oldest *...]
  transfers between devices with their start and end apart: 9 -> 11, of which waited for: 7 -> 8; matrix products, arithmetic and copies ran while one was open for 10% -> 14% of each run, Pallas kernels for 0% -> 0%
where the time goes in v1:
time: 790 us; the launch traced here: 785 us
  waiting for transfers between devices  628 us (79%)
  matrix products  81 us (10%)
  local copies, waits for them, and re-layouts  35.6 us (5%)
  other arithmetic  19.5 us (2%)
  between operations  13.7 us (2%)
    all_gather x1, waiting for transfers between devices, on_device(): lax.all_gather(w_gate, 'ctx', axis=0, tiled=True)  278 us
    all_gather x1, waiting for transfers between devices, on_device(): lax.all_gather(w_value, 'ctx', axis=0, tiled=True)  145 us
    ppermute x3, waiting for transfers between devices, on_device(): jax.lax.ppermute(field, 'tp', [(j0, (j0 + 1) % oldest) for j0 in range(ol...  121 us
    ppermute x6, waiting for transfers between devices, swapped(): lax.ppermute(value, axis, [(i, i ^ 1 << distance) for i in range(lax.axis...  81.2 us
    dot_general x1, matrix products, on_device(): jnp.dot(full_rows, lax.all_gather(w_value, 'ctx', axis=0, tiled=True), pr...  25.6 us
    dot_general x1, matrix products, on_device(): jnp.dot(full_rows, lax.all_gather(w_gate, 'ctx', axis=0, tiled=True), pre...  24.8 us
  transfers between devices with their start and end apart: 11, of which 8 were waited for; matrix products, arithmetic and copies ran while one was open for 14% of the time, Pallas kernels for 0%

profile of v1, /device:TPU:17, one launch (start us, length us, event | category | flops | bytes accessed | tf_op | source)
XLA Modules:
  0.0 785.4 jit_solution(15474561695922368310)
XLA Ops:
  6.5 0.7 all-gather.3.cloned.1.call-update
  7.3 0.7 all-gather.5.cloned.1.call-update
  8.0 1.3 collective-permute-start
  9.3 46.5 %collective-permute-done = bf16[512,2048]{1,0:T(8,128)(2,1)} collective-permute-done((bf16[512,2048]{1,0:T(8,128)(2,1)}, bf16[512,2048]{1,0:T(8,128)(2,1)}, u32[]{:S(2)}, u32[]{:S(2)}) %collective-permute-start) | collective-permute-done | bytes 2097184 | tf_op jit(solution)/shard_map/ppermute | solution.py:37
  56.1 1.2 reduce-window.6
  57.3 45.4 %collective-permute-done.1 = bf16[512,2048]{1,0:T(8,128)(2,1)} collective-permute-done((bf16[512,2048]{1,0:T(8,128)(2,1)}, bf16[512,2048]{1,0:T(8,128)(2,1)}, u32[]{:S(2)}, u32[]{:S(2)}) %collective-permute-start.1) | collective-permute-done | bytes 2097184 | tf_op jit(solution)/shard_map/ppermute | solution.py:37
  103.0 0.7 copy_bitcast_fusion.2
  103.9 1.7 fusion.20
  105.6 0.5 constant_dynamic-slice_fusion
  106.1 0.7 negate_exponential_fusion
  106.9 4.2 broadcast_in_dim.30
  111.1 1.5 constant_dynamic-update-slice_fusion.3
  112.6 3.2 constant_dynamic-update-slice_fusion.2
  115.8 3.3 constant_dynamic-update-slice_fusion.1
  119.1 29.6 %collective-permute-done.2 = bf16[512,2048]{1,0:T(8,128)(2,1)} collective-permute-done((bf16[512,2048]{1,0:T(8,128)(2,1)}, bf16[512,2048]{1,0:T(8,128)(2,1)}, u32[]{:S(2)}, u32[]{:S(2)}) %collective-permute-start.2) | collective-permute-done | bytes 2097184 | tf_op jit(solution)/shard_map/ppermute | solution.py:37
  148.7 3.2 constant_dynamic-update-slice_fusion
  151.9 145.3 %all-gather.3.cloned.1.call-done = bf16[8192,2048]{1,0:T(8,128)(2,1)} async-done(((bf16[1024,2048]{1,0:T(8,128)(2,1)}), bf16[8192,2048]{1,0:T(8,128)(2,1)}) %all-gather.3.cloned.1.call-update) | async-done | bytes 33554448 | tf_op jit(solution)/shard_map/all_gather | solution.py:43
  297.3 25.6 %convolution_convert_fusion.1 = bf16[512,2048]{1,0:T(8,128)(2,1)} fusion(bf16[512,8192]{1,0:T(8,128)(2,1)} %constant_dynamic-update-slice_fusion, bf16[8192,2048]{1,0:T(8,128)(2,1)} %all-gather.3.cloned.1.call-done), kind=kOutput, calls=%fused_computation.16 | convolution fusion | flops 17180917760 | bytes 44040192 | tf_op jit(solution)/shard_map/dot_general | solution.py:41
  322.9 2.9 copy.27
  325.8 1.3 copy-done.5
  327.1 4.0 fusion.2
  331.6 0.8 iota_compare_fusion
  332.4 1.8 constant_dynamic-slice_fusion.1
  334.1 0.8 slice_bitcast_fusion
  335.0 1.0 multiply_bitcast_fusion
  336.0 1.3 fusion.10
  337.4 2.9 collective-permute-done.6
  340.3 1.7 collective-permute-start.8
  342.1 2.1 collective-permute-done.8
  344.2 1.3 copy-done.3
  345.6 3.4 add_select_fusion.1
  349.0 3.0 collective-permute-start.5
  352.0 278.4 %all-gather.5.cloned.1.call-done = bf16[8192,2048]{1,0:T(8,128)(2,1)} async-done(((bf16[1024,2048]{1,0:T(8,128)(2,1)}), bf16[8192,2048]{1,0:T(8,128)(2,1)}) %all-gather.5.cloned.1.call-update) | async-done | bytes 33554448 | tf_op jit(solution)/shard_map/all_gather | solution.py:48
  630.4 24.8 %fusion.8 = f32[512,2048]{1,0:T(8,128)} fusion(bf16[512,8192]{1,0:T(8,128)(2,1)} %constant_dynamic-update-slice_fusion, bf16[8192,2048]{1,0:T(8,128)(2,1)} %all-gather.5.cloned.1.call-done), kind=kOutput, calls=%fused_computation.15 | convolution fusion | flops 17181966336 | bytes 46137344 | tf_op jit(solution)/shard_map/dot_general | solution.py:46
  655.2 5.3 copy.32
  660.5 2.2 add_select_fusion
  662.7 0.8 collective-permute-start.7
  663.5 10.7 %fusion = f32[32,64,512]{2,1,0:T(8,128)S(1)} fusion(bf16[512,32,64]{0,2,1:T(8,128)(2,1)S(1)} %bitcast.73, f32[512,512]{1,0:T(8,128)S(1)} %copy-done.10, f32[32,512]{1,0:T(8,128)S(1)} %copy-done.12, pred[512,512]{1,0:T(8,128)(4,1)S(1)} %copy-done.11), kind=kOutput, calls=%fused_computation.3 | convolution fusion | flops 1124073472 | bytes 7667712 | tf_op jit(solution)/shard_map/hts,shp->thp/dot_general | solution.py:66
  674.2 1.6 bitcast_dynamic-update-slice_fusion.3
  675.8 1.5 bitcast_dynamic-update-slice_fusion.2
  677.3 76.2 %collective-permute-done.7 = f32[32,64,256]{2,1,0:T(8,128)S(1)} collective-permute-done((f32[32,64,256]{2,1,0:T(8,128)S(1)}, f32[32,64,256]{2,1,0:T(8,128)S(1)}, u32[]{:S(2)}, u32[]{:S(2)}) %collective-permute-start.7) | collective-permute-done | bytes 2097184 | tf_op jit(solution)/shard_map/ppermute | solution.py:13
  753.5 1.6 bitcast_dynamic-update-slice_fusion.1
  755.1 1.6 broadcast_dynamic-update-slice_fusion
  756.7 1.6 bitcast_dynamic-update-slice_fusion
  758.3 14.6 %multiply_reduce_fusion = f32[512,32,64]{0,2,1:T(8,128)S(1)} fusion(f32[512,32,5]{0,1,2:T(8,128)S(1)} %multiply_bitcast_fusion, f32[5,32,64,256]{3,2,1,0:T(8,128)} %bitcast_dynamic-update-slice_fusion, bf16[512,1,1,256]{3,2,1,0:T(2,128)(2,1)S(1)} %constant_dynamic-slice_fusion.1), kind=kOutput, calls=%fused_computation.1 | convolution fusion | flops 16115564544 | bytes 15269888 | tf_op jit(solution)/shard_map/tn,lhpn->tlhp/dot_general | solution.py:98
  773.0 2.4 multiply_reduce_fusion.1
  775.5 0.7 multiply_convert_fusion.4
  776.1 2.4 copy.33
  (50 shorter events, 1.5 us)
Async XLA Ops:
  6.5 49.6 %copy-start = (f32[512,32]{0,1:T(8,128)S(1)}, f32[512,32]{0,1:T(8,128)}, u32[]{:S(2)}) copy-start(f32[512,32]{0,1:T(8,128)} %param.13) | copy-start | bytes 196612
  6.5 97.3 %copy-start.7 = (bf16[512,2,4,256]{3,2,1,0:T(4,128)(2,1)S(1)}, bf16[512,2,4,256]{3,2,1,0:T(4,128)(2,1)}, u32[]{:S(2)}) copy-start(bf16[512,2,4,256]{3,2,1,0:T(4,128)(2,1)} %param.12) | copy-start | bytes 6291460
  6.5 290.7 %all-gather.3.cloned.1.call-start = ((), (), s32[]{:S(2)}) async-start(), calls=%async_computation | async-start | bytes 37748736 | tf_op jit(solution)/shard_map/all_gather | solution.py:43
  7.3 623.1 %all-gather.5.cloned.1.call-start = ((), (), s32[]{:S(2)}) async-start(), calls=%async_computation.1 | async-start | bytes 37748736 | tf_op jit(solution)/shard_map/all_gather | solution.py:48
  8.0 47.8 %collective-permute-start = (bf16[512,2048]{1,0:T(8,128)(2,1)}, bf16[512,2048]{1,0:T(8,128)(2,1)}, u32[]{:S(2)}, u32[]{:S(2)}) collective-permute-start(bf16[512,2048]{1,0:T(8,128)(2,1)} %param.9), channel_id=1, source_target_pairs={{0,1},{1,2},{2,3},{3,0},{4,5},{5,6},{6,7},{7,4},{8,9},{9,10},{10,1... | collective-permute-start | bytes 6291464 | tf_op jit(solution)/shard_map/ppermute | solution.py:37
  55.8 46.9 %collective-permute-start.1 = (bf16[512,2048]{1,0:T(8,128)(2,1)}, bf16[512,2048]{1,0:T(8,128)(2,1)}, u32[]{:S(2)}, u32[]{:S(2)}) collective-permute-start(bf16[512,2048]{1,0:T(8,128)(2,1)} %collective-permute-done), channel_id=1, source_target_pairs={{0,1},{1,2},{2,3},{3,0},{4,5},{5,6},{6,7},{7,4},{8,9},{9,10},{10,1... | collective-permute-start | bytes 6291464 | tf_op jit(solution)/shard_map/ppermute | solution.py:37
  102.7 46.0 %collective-permute-start.2 = (bf16[512,2048]{1,0:T(8,128)(2,1)}, bf16[512,2048]{1,0:T(8,128)(2,1)}, u32[]{:S(2)}, u32[]{:S(2)}) collective-permute-start(bf16[512,2048]{1,0:T(8,128)(2,1)} %collective-permute-done.1), channel_id=1, source_target_pairs={{0,1},{1,2},{2,3},{3,0},{4,5},{5,6},{6,7},{7,4},{8,9},{9,10},{10,1... | collective-permute-start | bytes 6291464 | tf_op jit(solution)/shard_map/ppermute | solution.py:37
  106.9 4.3 copy-start.8
  325.8 1.3 copy-start.5
  327.1 15.0 %copy-start.13 = (f32[2048]{0:T(1024)S(1)}, f32[2048]{0:T(1024)}, u32[]{:S(2)}) copy-start(f32[2048]{0:T(1024)} %param.17) | copy-start | bytes 24580
  331.1 13.1 %collective-permute-start.3 = (f32[32,64,256]{2,1,0:T(8,128)}, f32[32,64,256]{2,1,0:T(8,128)S(1)}, u32[]{:S(2)}, u32[]{:S(2)}) collective-permute-start(f32[32,64,256]{2,1,0:T(8,128)} %fusion.2), channel_id=1, source_target_pairs={{0,4},{4,0},{8,12},{12,8},{16,20},{20,16},{24,28},{28,24},{1,5},{5... | collective-permute-start | bytes 6291464 | tf_op jit(solution)/shard_map/ppermute | solution.py:13
  331.3 6.0 collective-permute-start.4
  337.3 3.0 collective-permute-start.6
  340.3 3.9 collective-permute-start.8
  344.2 1.3 copy-start.3
  349.0 311.5 %collective-permute-start.5 = (f32[32,64,256]{2,1,0:T(8,128)}, f32[32,64,256]{2,1,0:T(8,128)S(1)}, u32[]{:S(2)}, u32[]{:S(2)}) collective-permute-start(f32[32,64,256]{2,1,0:T(8,128)} %add_select_fusion.1), channel_id=1, source_target_pairs={{0,8},{4,12},{8,0},{12,4},{16,24},{20,28},{24,16},{28,20},{1,9},{5... | collective-permute-start | bytes 6291464 | tf_op jit(solution)/shard_map/ppermute | solution.py:13
  660.5 3.0 copy-start.6
  660.5 3.0 copy-start.10
  660.5 3.0 copy-start.11
  660.5 3.0 copy-start.12
  662.7 90.8 %collective-permute-start.7 = (f32[32,64,256]{2,1,0:T(8,128)S(1)}, f32[32,64,256]{2,1,0:T(8,128)S(1)}, u32[]{:S(2)}, u32[]{:S(2)}) collective-permute-start(f32[32,64,256]{2,1,0:T(8,128)S(1)} %add_select_fusion), channel_id=1, source_target_pairs={{0,16},{4,20},{8,24},{12,28},{16,0},{20,4},{24,8},{28,12},{1,17},{... | collective-permute-start | bytes 6291464 | tf_op jit(solution)/shard_map/ppermute | solution.py:13
  663.5 10.7 %copy-start.4 = (f32[32,64,256]{2,1,0:T(8,128)S(1)}, f32[32,64,256]{2,1,0:T(8,128)}, u32[]{:S(2)}) copy-start(f32[32,64,256]{2,1,0:T(8,128)} %copy-done.3) | copy-start | bytes 6291460
  677.3 79.4 %copy-start.9 = (f32[32,64,256]{2,1,0:T(8,128)S(1)}, f32[32,64,256]{2,1,0:T(8,128)}, u32[]{:S(2)}) copy-start(f32[32,64,256]{2,1,0:T(8,128)} %param.15) | copy-start | bytes 6291460
  758.3 14.7 %copy-start.2 = (f32[512,2048]{0,1:T(8,128)S(1)}, f32[512,2048]{0,1:T(8,128)}, u32[]{:S(2)}) copy-start(f32[512,2048]{0,1:T(8,128)} %copy.32) | copy-start | bytes 12582916
  758.3 14.7 %copy-start.14 = (f32[32]{0:T(128)S(1)}, f32[32]{0:T(128)}, u32[]{:S(2)}) copy-start(f32[32]{0:T(128)} %param.16) | copy-start | bytes 388
  775.4 3.1 copy-start.1
Sparse Core Ops, SparseCore 0:
  8.9 288.2 all-gather.2
  298.8 331.5 all-gather.4
